TPU v7x, 256 devices: a whole 4x4x8 slice. The times are simulated.
256 devices in a mesh: blk: 64 (over y, z, core), pair: 4 (over x).
Axes of the slice: x: 4, y: 4, z: 8, core: 2. Of those that a mesh axis runs over, the one named last changes fastest.
Arguments:
- raw_strain: bfloat16 [4, 9216, 8192], P('pair', 'blk'), may hold values from -6 to 6
- aa_taps: bfloat16 [64], replicated, may hold values from -0.75 to 0.75
- white_taps: bfloat16 [255], replicated, may hold values from -0.375 to 0.375
- src_channels: int32 [64, 64], replicated, may hold values from 0 to 8191, as said below
- recv_lo: int32 [64, 64], P('blk'), may hold values from 0 to 63
- recv_hi: int32 [64, 64], P('blk'), may hold values from 65 to 128
Outputs:
- xcorr: float32 [64, 1024, 64, 128], P('blk', 'pair')
Inputs may be any that keep to these rules, and one draw needn't show every extreme that they name: `src_channels`: row b lists 64 distinct channels: exactly 2 channels from each of 32 distinct tiles and none from the other tiles; tile of channel c is c // 128.
All inputs are finite; a program needn't handle non-finite values.
Results may differ from a plain program's by a relative error of at most 0.0052.
Values may be sent and summed in bfloat16 or wider, within the bound.
A program may use at most 128 MiB of HBM per device.

v0:
```python
import math
import jax
import jax.numpy as jnp
from jax import lax
from jax.sharding import PartitionSpec as P

DECIM = 8
KA = 64
LAGS = 1024
CAP = 2


def extended_2(cells, sides, width):
    for axis, dim in sides:
        count = lax.axis_size(axis)
        ends = count - 1
        head = lax.slice_in_dim(cells, 0, width, axis=dim)
        tail = lax.slice_in_dim(cells, cells.shape[dim] - width, cells.shape[dim], axis=dim)
        cells = jnp.concatenate(
            [
                lax.ppermute(tail, axis, [(i, (i + 1) % count) for i in range(ends)]),
                cells,
                lax.ppermute(head, axis, [((i + 1) % count, i) for i in range(ends)]),
            ],
            axis=dim,
        )
    return cells


def whiten_matrix(white_taps, length):
    n_taps = white_taps.shape[0]
    half = n_taps // 2
    left = length - 1 - half
    right = 2 * length - 1 - left - n_taps
    spread = jnp.pad(white_taps, (left, right))
    rolled = jnp.roll(spread, length)
    tiled = jnp.tile(rolled, length)[: length * (2 * length - 2)]
    return tiled.reshape(length, 2 * length - 2)[:, :length]


def body(raw_strain, aa_taps, white_taps, src_channels, recv_lo, recv_hi):
    raw_len = raw_strain.shape[1]
    short_len = raw_len // DECIM
    channels = raw_strain.shape[2]
    n_blocks = lax.axis_size("blk")
    tile = channels // n_blocks
    seg_len = short_len * n_blocks
    span = seg_len - LAGS
    extended = extended_2(raw_strain[0], (("blk", 0),), KA // 2)
    out_rows = jnp.arange(short_len)[:, None]
    in_cols = jnp.arange(raw_len + KA)[None, :]
    offset = in_cols - DECIM * out_rows
    valid = (offset >= 0) & (offset < KA)
    aa_matrix = jnp.where(valid, aa_taps[jnp.clip(offset, 0, KA - 1)], jnp.zeros((), aa_taps.dtype))
    decimated = jnp.dot(aa_matrix, extended, preferred_element_type=jnp.float32).astype(
        jnp.bfloat16
    )
    white_matrix = whiten_matrix(white_taps, seg_len)
    n_src = src_channels.shape[1]
    n_tiles = src_channels.shape[0]
    tile_raw = lax.all_to_all(decimated, "blk", split_axis=1, concat_axis=0, tiled=True)
    white_tile = jnp.dot(white_matrix, tile_raw, preferred_element_type=jnp.float32).astype(
        jnp.bfloat16
    )
    tile_of = src_channels // tile
    chan_of = src_channels - tile_of * tile
    same = tile_of[:, :, None] == tile_of[:, None, :]
    earlier = jnp.arange(n_src)[None, :] < jnp.arange(n_src)[:, None]
    slot_of = jnp.sum((same & earlier[None]).astype(jnp.int32), axis=2)
    mine = lax.axis_index("blk")
    belongs = tile_of == mine
    one_slot = (slot_of[:, :, None] == jnp.arange(CAP)[None, None, :]) & belongs[:, :, None]
    one_chan = chan_of[:, :, None] == jnp.arange(tile)[None, None, :]
    picker = jnp.einsum(
        "dkc,dkr->dcr",
        one_slot.astype(jnp.bfloat16),
        one_chan.astype(jnp.bfloat16),
        preferred_element_type=jnp.float32,
    ).astype(jnp.bfloat16)
    outgoing = jnp.einsum(
        "dcr,tr->dct", picker, white_tile, preferred_element_type=jnp.float32
    ).astype(jnp.bfloat16)
    incoming = lax.all_to_all(outgoing, "blk", split_axis=0, concat_axis=0, tiled=True)
    own_tiles = lax.dynamic_index_in_dim(tile_of, mine, 0, keepdims=False)
    own_slots = lax.dynamic_index_in_dim(slot_of, mine, 0, keepdims=False)
    selector = (own_tiles[:, None, None] == jnp.arange(n_tiles)[None, :, None]) & (
        own_slots[:, None, None] == jnp.arange(CAP)[None, None, :]
    )
    sources = jnp.einsum(
        "kec,ect->tk", selector.astype(jnp.bfloat16), incoming, preferred_element_type=jnp.float32
    ).astype(jnp.bfloat16)
    source_window = sources[LAGS // 2 : LAGS // 2 + span]
    lag_share = LAGS // lax.axis_size("pair")
    lag_start = lax.axis_index("pair") * lag_share
    lag_block = math.gcd(128, lag_share)
    n_lag_blocks = lag_share // lag_block
    initial = jnp.zeros((lag_share, n_src, tile), jnp.float32)
    total = initial
    tiles_in = lax.all_gather(white_tile[None], "pair", axis=0, tiled=True)
    sources_in = lax.all_gather(source_window[None], "pair", axis=0, tiled=True)
    for segment in range(tiles_in.shape[0]):
        window = lax.dynamic_slice_in_dim(tiles_in[segment], lag_start, span + lag_share, 0)
        parts = []
        for block in range(n_lag_blocks):
            base = block * lag_block
            hankel = jnp.stack(
                [window[base + shift : base + shift + span] for shift in range(lag_block)], 1
            )
            parts.append(
                jnp.einsum(
                    "tk,tjr->jkr", sources_in[segment], hankel, preferred_element_type=jnp.float32
                )
            )
        total = total + jnp.concatenate(parts, 0)
    scale = 1.0 / math.sqrt(span * lax.axis_size("pair"))
    position = jnp.arange(tile)[None, :]
    inside = (position >= recv_lo[0][:, None]) & (position < recv_hi[0][:, None])
    mask = jnp.where(inside, jnp.float32(scale), jnp.float32(0.0))
    return (total * mask[None])[None]


def solution(mesh):
    placed = (P("pair", "blk", None), P(), P(), P(), P("blk", None), P("blk", None))
    return jax.shard_map(
        body, mesh=mesh, in_specs=placed, out_specs=P("blk", "pair", None, None), check_vma=False
    )
```

profile of v0, /device:TPU:2, one launch (start us, length us, event | category | flops | bytes accessed | tf_op | source)
XLA Modules:
  0.0 203.3 jit_solution(10262311969563306636)
XLA Ops:
  6.5 1.3 slice_bitcast_fusion.1
  7.8 1.8 collective-permute-start
  9.6 1.3 collective-permute-start.1
  11.1 21.4 %gather_fusion = bf16[3744]{0:T(1024)(128)(2,1)S(1)} fusion(bf16[64]{0:T(256)(128)(2,1)S(1)} %copy-done, s32[4096]{0:T(1024)S(1)} %pad_clamp_fusion), kind=kCustom, calls=%fused_computation | custom fusion | bytes 29952 | tf_op jit(solution)/shard_map/gather | solution.py:54
  32.6 2.3 %convolution_convert_fusion = bf16[18,8192]{1,0:T(8,128)(2,1)S(1)} fusion(bf16[32,8192]{1,0:T(8,128)(2,1)S(1)} %collective-permute-done.1, bf16[144,8192]{1,0:T(8,128)(2,1)} %bitcast.4185, bf16[32,8192]{1,0:T(8,128)(2,1)S(1)} %collective-permute-done, bf16[18,208]{1,0:T(8,128)(2,1)S(1)} %reshape.2336, s32[18]{0:T(128)S(1)} %iota_multiply_fusion), kind=kOutput, calls=%fused_computation.1 | convolution fusion | flops 71731488 | bytes 3710344 | tf_op jit(solution)/shard_map/dot_general | solution.py:55
  35.0 1.0 copy.12
  36.0 15.8 %all-to-all-start = ((bf16[18,64,128]{2,0,1:T(8,128)(2,1)}), bf16[18,64,128]{2,0,1:T(8,128)(2,1)S(1)}, u32[]{:S(2)}, u32[]{:S(2)}) async-start(bf16[18,64,128]{2,0,1:T(8,128)(2,1)} %copy.12), calls=%async_computation | async-start | bytes 786432 | tf_op jit(solution)/shard_map/all_to_all | solution.py:61
  51.8 0.6 all-gather.4.cloned.1.call-start
  52.5 2.7 %tile.4 = bf16[1152,2303]{1,0:T(8,128)(2,1)} broadcast(bf16[2303]{0:T(1024)(128)(2,1)S(1)} %pad_maximum_fusion), dimensions={1} | broadcast | bytes 5310718 | tf_op jit(solution)/shard_map/tile | solution.py:37
  55.2 14.8 %tile.10 = bf16[2653056]{0:T(1024)(128)(2,1)} reshape(bf16[1152,2303]{1,0:T(8,128)(2,1)} %tile.4) | data formatting | bytes 10612224 | tf_op jit(solution)/shard_map/tile | solution.py:37
  70.0 5.8 %slice.5204 = bf16[2651904]{0:T(1024)(128)(2,1)} slice(bf16[2653056]{0:T(1024)(128)(2,1)} %tile.10), slice={[0:2651904]} | slice | bytes 10607616 | tf_op jit(solution)/shard_map/slice | solution.py:37
  75.8 13.2 %reshape.2334 = bf16[1152,2302]{1,0:T(8,128)(2,1)} reshape(bf16[2651904]{0:T(1024)(128)(2,1)} %slice.5204) | data formatting | bytes 10607616 | tf_op jit(solution)/shard_map/reshape | solution.py:38
  89.1 3.3 %fusion.10 = bf16[1152,128]{1,0:T(8,128)(2,1)} fusion(bf16[1152,128]{1,0:T(8,128)(2,1)S(1)} %all_to_all.20, bf16[1152,2302]{1,0:T(8,128)(2,1)} %reshape.2334), kind=kOutput, calls=%fused_computation.13 | convolution fusion | flops 339886080 | bytes 3244032 | tf_op jit(solution)/shard_map/dot_general | solution.py:62
  92.5 1.9 convert_reduce_fusion
  94.4 0.9 fusion.14
  95.3 1.2 convolution_convert_fusion.1
  96.6 1.0 copy.14
  97.6 10.3 %all-to-all-start.1 = ((bf16[64,2,1152]{2,1,0:T(2,128)(2,1)}), bf16[64,2,1152]{2,1,0:T(2,128)(2,1)S(1)}, u32[]{:S(2)}, u32[]{:S(2)}) async-start(bf16[64,2,1152]{2,1,0:T(2,128)(2,1)} %copy.14), calls=%async_computation.1 | async-start | bytes 589824 | tf_op jit(solution)/shard_map/all_to_all | solution.py:83
  108.1 12.4 %all-to-all-done.1 = bf16[64,2,1152]{2,1,0:T(2,128)(2,1)S(1)} async-done(((bf16[64,2,1152]{2,1,0:T(2,128)(2,1)}), bf16[64,2,1152]{2,1,0:T(2,128)(2,1)S(1)}, u32[]{:S(2)}, u32[]{:S(2)}) %all-to-all-start.1) | async-done | bytes 294944 | tf_op jit(solution)/shard_map/all_to_all | solution.py:83
  120.5 0.3 convolution_bitcast_fusion
  120.8 11.2 %all-gather.1 = bf16[512,64]{0,1:T(8,128)(2,1)S(1)} all-gather(bf16[128,64]{0,1:T(8,128)(2,1)S(1)} %slice.9333), channel_id=3, replica_groups=mesh['blk'=64,'pair'=4] {'pair'}, dimensions={0}, use_global_device_ids=true | all-gather | bytes 81920 | tf_op jit(solution)/shard_map/all_gather | solution.py:100
  132.0 1.3 fusion.44
  139.6 2.7 %convolution_bitcast_fusion.1 = f32[1,128,64,128]{3,2,1,0:T(8,128)} fusion(bf16[128,128,128]{2,0,1:T(8,128)(2,1)S(1)} %constant_dynamic-update-slice_fusion.896, bf16[512,64]{0,1:T(8,128)(2,1)S(1)} %all-gather.1), kind=kOutput, calls=%fused_computation.16 | convolution fusion | flops 268435456 | bytes 8404992 | tf_op jit(solution)/shard_map/tk,tjr->jkr/dot_general | solution.py:110
  142.3 2.6 %convolution_bitcast_fusion.2 = f32[1,128,64,128]{3,2,1,0:T(8,128)} fusion(bf16[128,128,128]{2,0,1:T(8,128)(2,1)S(1)} %constant_dynamic-update-slice_fusion.768, bf16[512,64]{0,1:T(8,128)(2,1)S(1)} %all-gather.1), kind=kOutput, calls=%fused_computation.17 | convolution fusion | flops 268435456 | bytes 8404992 | tf_op jit(solution)/shard_map/tk,tjr->jkr/dot_general | solution.py:110
  148.0 2.7 %convolution_bitcast_fusion.3 = f32[1,128,64,128]{3,2,1,0:T(8,128)} fusion(bf16[128,128,128]{2,0,1:T(8,128)(2,1)S(1)} %constant_dynamic-update-slice_fusion.640, bf16[512,64]{0,1:T(8,128)(2,1)S(1)} %all-gather.1), kind=kOutput, calls=%fused_computation.18 | convolution fusion | flops 268435456 | bytes 8404992 | tf_op jit(solution)/shard_map/tk,tjr->jkr/dot_general | solution.py:110
  153.2 0.4 constant_dynamic-update-slice_fusion.532
  154.1 2.7 %convolution_bitcast_fusion.4 = f32[1,128,64,128]{3,2,1,0:T(8,128)} fusion(bf16[128,128,128]{2,0,1:T(8,128)(2,1)S(1)} %constant_dynamic-update-slice_fusion.512, bf16[512,64]{0,1:T(8,128)(2,1)S(1)} %all-gather.1), kind=kOutput, calls=%fused_computation.19 | convolution fusion | flops 268435456 | bytes 8404992 | tf_op jit(solution)/shard_map/tk,tjr->jkr/dot_general | solution.py:110
  159.8 2.7 %convolution_bitcast_fusion.5 = f32[1,128,64,128]{3,2,1,0:T(8,128)} fusion(bf16[128,128,128]{2,0,1:T(8,128)(2,1)S(1)} %constant_dynamic-update-slice_fusion.384, bf16[512,64]{0,1:T(8,128)(2,1)S(1)} %all-gather.1), kind=kOutput, calls=%fused_computation.20 | convolution fusion | flops 268435456 | bytes 8404992 | tf_op jit(solution)/shard_map/tk,tjr->jkr/dot_general | solution.py:110
  165.6 2.6 %convolution_bitcast_fusion.6 = f32[1,128,64,128]{3,2,1,0:T(8,128)} fusion(bf16[128,128,128]{2,0,1:T(8,128)(2,1)S(1)} %constant_dynamic-update-slice_fusion.256, bf16[512,64]{0,1:T(8,128)(2,1)S(1)} %all-gather.1), kind=kOutput, calls=%fused_computation.21 | convolution fusion | flops 268435456 | bytes 8404992 | tf_op jit(solution)/shard_map/tk,tjr->jkr/dot_general | solution.py:110
  171.2 2.7 %convolution_bitcast_fusion.7 = f32[1,128,64,128]{3,2,1,0:T(8,128)} fusion(bf16[128,128,128]{2,0,1:T(8,128)(2,1)S(1)} %constant_dynamic-update-slice_fusion.128, bf16[512,64]{0,1:T(8,128)(2,1)S(1)} %all-gather.1), kind=kOutput, calls=%fused_computation.22 | convolution fusion | flops 268435456 | bytes 8404992 | tf_op jit(solution)/shard_map/tk,tjr->jkr/dot_general | solution.py:110
  177.1 2.7 %convolution_bitcast_fusion.8 = f32[1,128,64,128]{3,2,1,0:T(8,128)} fusion(bf16[128,128,128]{2,0,1:T(8,128)(2,1)S(1)} %constant_dynamic-update-slice_fusion, bf16[512,64]{0,1:T(8,128)(2,1)S(1)} %all-gather.1), kind=kOutput, calls=%fused_computation.23 | convolution fusion | flops 268435456 | bytes 8404992 | tf_op jit(solution)/shard_map/tk,tjr->jkr/dot_general | solution.py:110
  179.8 16.4 %fusion.2 = f32[1,256,64,128]{3,2,1,0:T(8,128)} fusion(f32[1,128,64,128]{3,2,1,0:T(8,128)} %convolution_bitcast_fusion.7, f32[1,128,64,128]{3,2,1,0:T(8,128)} %convolution_bitcast_fusion.8, f32[1,128,64,128]{3,2,1,0:T(8,128)} %convolution_bitcast_fusion.5, f32[1,128,64,128]{3,2,1,0:T(8,128)} %convolution_bitcast_fusion.6, ...), kind=kLoop, calls=%fused_computation.5 | loop fusion | flops 16777216 | bytes 41975808 | tf_op jit(solution)/shard_map/mul | solution.py:119
  (1061 shorter events, 21.2 us)
Async XLA Ops:
  6.5 4.6 %copy-start = (bf16[64]{0:T(256)(128)(2,1)S(1)}, bf16[64]{0:T(256)(128)(2,1)}, u32[]{:S(2)}) copy-start(bf16[64]{0:T(256)(128)(2,1)} %param.7) | copy-start | bytes 388
  7.8 24.7 %collective-permute-start = (bf16[32,8192]{1,0:T(8,128)(2,1)S(1)}, bf16[32,8192]{1,0:T(8,128)(2,1)S(1)}, u32[]{:S(2)}, u32[]{:S(2)}) collective-permute-start(bf16[32,8192]{1,0:T(8,128)(2,1)S(1)} %get-tuple-element.5), channel_id=1, source_target_pairs={{0,4},{4,8},{8,12},{12,16},{16,20},{20,24},{24,28},{28,32},{32,36}... | collective-permute-start | bytes 1572872 | tf_op jit(solution)/shard_map/ppermute | solution.py:21
  9.6 23.0 %collective-permute-start.1 = (bf16[32,8192]{1,0:T(8,128)(2,1)S(1)}, bf16[32,8192]{1,0:T(8,128)(2,1)S(1)}, u32[]{:S(2)}, u32[]{:S(2)}) collective-permute-start(bf16[32,8192]{1,0:T(8,128)(2,1)S(1)} %get-tuple-element.6), channel_id=1, source_target_pairs={{4,0},{8,4},{12,8},{16,12},{20,16},{24,20},{28,24},{32,28},{36,32}... | collective-permute-start | bytes 1572872 | tf_op jit(solution)/shard_map/ppermute | solution.py:23
  32.6 19.8 %copy-start.3 = (bf16[255]{0:T(256)(128)(2,1)S(1)}, bf16[255]{0:T(256)(128)(2,1)}, u32[]{:S(2)}) copy-start(bf16[255]{0:T(256)(128)(2,1)} %param.8) | copy-start | bytes 1534
  36.0 53.0 %all-to-all-start = ((bf16[18,64,128]{2,0,1:T(8,128)(2,1)}), bf16[18,64,128]{2,0,1:T(8,128)(2,1)S(1)}, u32[]{:S(2)}, u32[]{:S(2)}) async-start(bf16[18,64,128]{2,0,1:T(8,128)(2,1)} %copy.12), calls=%async_computation | async-start | bytes 786432 | tf_op jit(solution)/shard_map/all_to_all | solution.py:61
  51.8 80.2 %all-gather.4.cloned.1.call-start = ((), (), s32[]{:S(2)}) async-start(), calls=%async_computation.2 | async-start | bytes 1474560 | tf_op jit(solution)/shard_map/all_gather | solution.py:99
  75.8 13.2 %copy-start.2 = (s32[64,64]{1,0:T(8,128)S(1)}, s32[64,64]{1,0:T(8,128)}, u32[]{:S(2)}) copy-start(s32[64,64]{1,0:T(8,128)} %param.9) | copy-start | bytes 49156
  88.9 19.0 %copy-start.4 = (s32[1,64]{1,0:T(1,128)S(1)}, s32[1,64]{1,0:T(1,128)}, u32[]{:S(2)}) copy-start(s32[1,64]{1,0:T(1,128)} %param.11) | copy-start | bytes 772
  88.9 19.1 %copy-start.5 = (s32[1,64]{1,0:T(1,128)S(1)}, s32[1,64]{1,0:T(1,128)}, u32[]{:S(2)}) copy-start(s32[1,64]{1,0:T(1,128)} %param.10) | copy-start | bytes 772
  97.6 22.9 %all-to-all-start.1 = ((bf16[64,2,1152]{2,1,0:T(2,128)(2,1)}), bf16[64,2,1152]{2,1,0:T(2,128)(2,1)S(1)}, u32[]{:S(2)}, u32[]{:S(2)}) async-start(bf16[64,2,1152]{2,1,0:T(2,128)(2,1)} %copy.14), calls=%async_computation.1 | async-start | bytes 589824 | tf_op jit(solution)/shard_map/all_to_all | solution.py:83
  179.8 16.4 %copy-start.1 = (bf16[64]{0:T(256)(128)(2,1)S(1)}, bf16[64]{0:T(256)(128)(2,1)}, u32[]{:S(2)}) copy-start(bf16[64]{0:T(256)(128)(2,1)} %param.7) | copy-start | bytes 388
Sparse Core Ops, SparseCore 0:
  92.6 27.0 all-gather.3
where the time goes:
time: 206 us; the launch traced here: 203 us
  local copies, waits for them, and re-layouts  83.7 us (41%)
  starting transfers between devices  29.8 us (14%)
  matrix products  29.4 us (14%)
  other arithmetic  18.6 us (9%)
  between operations  18.3 us (9%)
  waiting for transfers between devices  12.4 us (6%)
  blocking collectives  11.2 us (5%)
    gather x2, local copies, waits for them, and re-layouts, body(): aa_taps[jnp.clip(offset, 0, KA - 1)]  21.5 us
    dot_general x8, matrix products, body(): jnp.einsum('tk,tjr->jkr', sources_in[segment], hankel, preferred_element_...  21.4 us
    unnamed x1029, local copies, waits for them, and re-layouts  20.7 us
    another operation x2, local copies, waits for them, and re-layouts, whiten_matrix(): tiled = jnp.tile(rolled, length)[:length * (2 * length - 2)]  17.5 us
    mul x1, other arithmetic, body(): return (total * mask[None])[None]  16.4 us
    all_to_all x1, starting transfers between devices, body(): lax.all_to_all(decimated, 'blk', split_axis=1, concat_axis=0, tiled=True)  15.8 us
    reshape x1, local copies, waits for them, and re-layouts, whiten_matrix(): return tiled.reshape(length, 2 * length - 2)[:, :length]  13.2 us
    all_to_all x1, waiting for transfers between devices, body(): lax.all_to_all(outgoing, 'blk', split_axis=0, concat_axis=0, tiled=True)  12.4 us
  transfers between devices with their start and end apart: 5, of which 1 were waited for; matrix products, arithmetic and copies ran while one was open for 31% of the time, Pallas kernels for 0%

commit v1 on v0

--- a/solution.py
+++ b/solution.py
@@ -3,6 +3,7 @@
 import jax.numpy as jnp
 from jax import lax
 from jax.sharding import PartitionSpec as P
+from jax.lax import all_to_all, axis_size
 
 DECIM = 8
 KA = 64
@@ -97,7 +98,20 @@
     initial = jnp.zeros((lag_share, n_src, tile), jnp.float32)
     total = initial
     tiles_in = lax.all_gather(white_tile[None], "pair", axis=0, tiled=True)
-    sources_in = lax.all_gather(source_window[None], "pair", axis=0, tiled=True)
+
+    def tell_cubes(target):
+        piece_out = jnp.concatenate(
+            all_to_all(
+                jnp.stack([target for _ in range(axis_size("pair"))]),
+                axis_name="pair",
+                split_axis=0,
+                concat_axis=0,
+            ),
+            0,
+        )
+        return piece_out
+
+    sources_in = tell_cubes(source_window[None])
     for segment in range(tiles_in.shape[0]):
         window = lax.dynamic_slice_in_dim(tiles_in[segment], lag_start, span + lag_share, 0)
         parts = []

time: 206 us -> 365 us (1.77)
  local copies, waits for them, and re-layouts: 83.7 us -> 241 us
  blocking collectives: 11.2 us -> 0 us
  matrix products: 29.4 us -> 36.7 us
  starting transfers between devices: 29.8 us -> 34.8 us
    unnamed x1029 -> x1051, local copies, waits for them, and re-layouts: 20.7 us -> 176 us
    all_gather x1 -> x0, blocking collectives: 11.2 us -> none  [body(): sources_in = lax.all_gather(source_window[None], 'pair', axis=0, tiled=True)]
    dot_general x8, matrix products: 21.4 us -> 28.7 us  [body(): jnp.einsum('tk,tjr->jkr', sources_in[segment], hankel, preferred_element_...]
    all_to_all x0 -> x1, starting transfers between devices: none -> 5.01 us  [tell_cubes(): all_to_all(jnp.stack([target for _ in range(axis_size('pair'))]), axis_na...]
  transfers between devices with their start and end apart: 5 -> 6, of which waited for: 1 -> 1; matrix products, arithmetic and copies ran while one was open for 31% -> 67% of each run, Pallas kernels for 0% -> 0%
where the time goes in v1:
time: 365 us; the launch traced here: 361 us
  local copies, waits for them, and re-layouts  241 us (66%)
  matrix products  36.7 us (10%)
  starting transfers between devices  34.8 us (10%)
  other arithmetic  18.6 us (5%)
  between operations  17.4 us (5%)
  waiting for transfers between devices  12.4 us (3%)
    unnamed x1051, local copies, waits for them, and re-layouts  176 us
    dot_general x8, matrix products, body(): jnp.einsum('tk,tjr->jkr', sources_in[segment], hankel, preferred_element_...  28.7 us
    gather x2, local copies, waits for them, and re-layouts, body(): aa_taps[jnp.clip(offset, 0, KA - 1)]  21.5 us
    another operation x2, local copies, waits for them, and re-layouts, whiten_matrix(): tiled = jnp.tile(rolled, length)[:length * (2 * length - 2)]  17.6 us
    mul x1, other arithmetic, body(): return (total * mask[None])[None]  16.4 us
    all_to_all x1, starting transfers between devices, body(): lax.all_to_all(decimated, 'blk', split_axis=1, concat_axis=0, tiled=True)  15.8 us
    reshape x1, local copies, waits for them, and re-layouts, whiten_matrix(): return tiled.reshape(length, 2 * length - 2)[:, :length]  13.2 us
    all_to_all x1, waiting for transfers between devices, body(): lax.all_to_all(outgoing, 'blk', split_axis=0, concat_axis=0, tiled=True)  12.4 us
  transfers between devices with their start and end apart: 6, of which 1 were waited for; matrix products, arithmetic and copies ran while one was open for 67% of the time, Pallas kernels for 0%

profile of v1, /device:TPU:2, one launch (start us, length us, event | category | flops | bytes accessed | tf_op | source)
XLA Modules:
  0.0 361.1 jit_solution(4460731010223978534)
XLA Ops:
  6.5 1.3 slice_bitcast_fusion.1
  7.8 1.8 collective-permute-start
  9.6 1.3 collective-permute-start.1
  11.1 21.4 %gather_fusion = bf16[3744]{0:T(1024)(128)(2,1)S(1)} fusion(bf16[64]{0:T(256)(128)(2,1)S(1)} %copy-done, s32[4096]{0:T(1024)S(1)} %pad_clamp_fusion), kind=kCustom, calls=%fused_computation | custom fusion | bytes 29952 | tf_op jit(solution)/shard_map/gather | solution.py:55
  32.6 2.3 convolution_convert_fusion
  35.0 1.0 copy.12
  36.0 15.8 %all-to-all-start = ((bf16[18,64,128]{2,0,1:T(8,128)(2,1)}), bf16[18,64,128]{2,0,1:T(8,128)(2,1)S(1)}, u32[]{:S(2)}, u32[]{:S(2)}) async-start(bf16[18,64,128]{2,0,1:T(8,128)(2,1)} %copy.12), calls=%async_computation | async-start | bytes 786432 | tf_op jit(solution)/shard_map/all_to_all | solution.py:62
  52.5 2.7 tile.4
  55.2 14.8 %tile.10 = bf16[2653056]{0:T(1024)(128)(2,1)} reshape(bf16[1152,2303]{1,0:T(8,128)(2,1)} %tile.4) | data formatting | bytes 10612224 | tf_op jit(solution)/shard_map/tile | solution.py:38
  70.0 5.8 %slice.5204 = bf16[2651904]{0:T(1024)(128)(2,1)} slice(bf16[2653056]{0:T(1024)(128)(2,1)} %tile.10), slice={[0:2651904]} | slice | bytes 10607616 | tf_op jit(solution)/shard_map/slice | solution.py:38
  75.8 13.2 %reshape.2345 = bf16[1152,2302]{1,0:T(8,128)(2,1)} reshape(bf16[2651904]{0:T(1024)(128)(2,1)} %slice.5204) | data formatting | bytes 10607616 | tf_op jit(solution)/shard_map/reshape | solution.py:39
  89.2 3.3 fusion.10
  92.5 1.9 convert_reduce_fusion
  94.5 0.9 fusion.14
  95.4 1.2 convolution_convert_fusion.1
  96.6 1.0 copy.14
  97.6 10.3 %all-to-all-start.1 = ((bf16[64,2,1152]{2,1,0:T(2,128)(2,1)}), bf16[64,2,1152]{2,1,0:T(2,128)(2,1)S(1)}, u32[]{:S(2)}, u32[]{:S(2)}) async-start(bf16[64,2,1152]{2,1,0:T(2,128)(2,1)} %copy.14), calls=%async_computation.1 | async-start | bytes 589824 | tf_op jit(solution)/shard_map/all_to_all | solution.py:84
  108.1 12.4 %all-to-all-done.1 = bf16[64,2,1152]{2,1,0:T(2,128)(2,1)S(1)} async-done(((bf16[64,2,1152]{2,1,0:T(2,128)(2,1)}), bf16[64,2,1152]{2,1,0:T(2,128)(2,1)S(1)}, u32[]{:S(2)}, u32[]{:S(2)}) %all-to-all-start.1) | async-done | bytes 294944 | tf_op jit(solution)/shard_map/all_to_all | solution.py:84
  121.5 5.0 %all-to-all-start.2 = ((bf16[4,1,128,64]{2,3,1,0:T(8,128)(2,1)}), bf16[4,1,128,64]{2,3,1,0:T(8,128)(2,1)S(1)}, u32[]{:S(2)}, u32[]{:S(2)}) async-start(bf16[4,1,128,64]{2,3,1,0:T(8,128)(2,1)} %stack.3228), calls=%async_computation.2 | async-start | bytes 131072 | tf_op jit(solution)/shard_map/all_to_all | solution.py:104
  126.5 1.3 fusion.44
  148.8 1.1 constant_dynamic-update-slice_fusion.253
  305.9 5.0 %convolution_bitcast_fusion.1 = f32[1,128,64,128]{3,2,1,0:T(8,128)} fusion(bf16[128,128,128]{2,0,1:T(8,128)(2,1)} %copy-done.12, bf16[4,1,128,64]{2,3,1,0:T(8,128)(2,1)S(1)} %all-to-all-done.2), kind=kOutput, calls=%fused_computation.16 | convolution fusion | flops 268435456 | bytes 8404992 | tf_op jit(solution)/shard_map/tk,tjr->jkr/dot_general | solution.py:124
  310.9 2.8 convolution_bitcast_fusion.2
  313.7 0.8 copy-done.9
  314.4 2.8 convolution_bitcast_fusion.3
  317.2 0.8 copy-done.7
  318.0 2.8 convolution_bitcast_fusion.4
  321.5 2.8 convolution_bitcast_fusion.5
  325.0 2.9 convolution_bitcast_fusion.6
  327.9 4.9 %convolution_bitcast_fusion.7 = f32[1,128,64,128]{3,2,1,0:T(8,128)} fusion(bf16[128,128,128]{2,0,1:T(8,128)(2,1)} %constant_dynamic-update-slice_fusion.128, bf16[4,1,128,64]{2,3,1,0:T(8,128)(2,1)S(1)} %all-to-all-done.2), kind=kOutput, calls=%fused_computation.22 | convolution fusion | flops 268435456 | bytes 8404992 | tf_op jit(solution)/shard_map/tk,tjr->jkr/dot_general | solution.py:124
  332.7 4.9 %convolution_bitcast_fusion.8 = f32[1,128,64,128]{3,2,1,0:T(8,128)} fusion(bf16[128,128,128]{2,0,1:T(8,128)(2,1)} %constant_dynamic-update-slice_fusion, bf16[4,1,128,64]{2,3,1,0:T(8,128)(2,1)S(1)} %all-to-all-done.2), kind=kOutput, calls=%fused_computation.23 | convolution fusion | flops 268435456 | bytes 8404992 | tf_op jit(solution)/shard_map/tk,tjr->jkr/dot_general | solution.py:124
  337.7 16.4 %fusion.2 = f32[1,256,64,128]{3,2,1,0:T(8,128)} fusion(f32[1,128,64,128]{3,2,1,0:T(8,128)} %convolution_bitcast_fusion.7, f32[1,128,64,128]{3,2,1,0:T(8,128)} %convolution_bitcast_fusion.8, f32[1,128,64,128]{3,2,1,0:T(8,128)} %convolution_bitcast_fusion.5, f32[1,128,64,128]{3,2,1,0:T(8,128)} %convolution_bitcast_fusion.6, ...), kind=kLoop, calls=%fused_computation.5 | loop fusion | flops 16777216 | bytes 41975808 | tf_op jit(solution)/shard_map/mul | solution.py:133
  (1085 shorter events, 177.3 us)
Async XLA Ops:
  6.5 4.6 %copy-start = (bf16[64]{0:T(256)(128)(2,1)S(1)}, bf16[64]{0:T(256)(128)(2,1)}, u32[]{:S(2)}) copy-start(bf16[64]{0:T(256)(128)(2,1)} %param.7) | copy-start | bytes 388
  7.8 24.7 %collective-permute-start = (bf16[32,8192]{1,0:T(8,128)(2,1)S(1)}, bf16[32,8192]{1,0:T(8,128)(2,1)S(1)}, u32[]{:S(2)}, u32[]{:S(2)}) collective-permute-start(bf16[32,8192]{1,0:T(8,128)(2,1)S(1)} %get-tuple-element.5), channel_id=1, source_target_pairs={{0,4},{4,8},{8,12},{12,16},{16,20},{20,24},{24,28},{28,32},{32,36}... | collective-permute-start | bytes 1572872 | tf_op jit(solution)/shard_map/ppermute | solution.py:22
  9.6 23.0 %collective-permute-start.1 = (bf16[32,8192]{1,0:T(8,128)(2,1)S(1)}, bf16[32,8192]{1,0:T(8,128)(2,1)S(1)}, u32[]{:S(2)}, u32[]{:S(2)}) collective-permute-start(bf16[32,8192]{1,0:T(8,128)(2,1)S(1)} %get-tuple-element.6), channel_id=1, source_target_pairs={{4,0},{8,4},{12,8},{16,12},{20,16},{24,20},{28,24},{32,28},{36,32}... | collective-permute-start | bytes 1572872 | tf_op jit(solution)/shard_map/ppermute | solution.py:24
  32.6 19.8 %copy-start.14 = (bf16[255]{0:T(256)(128)(2,1)S(1)}, bf16[255]{0:T(256)(128)(2,1)}, u32[]{:S(2)}) copy-start(bf16[255]{0:T(256)(128)(2,1)} %param.8) | copy-start | bytes 1534
  36.0 53.1 %all-to-all-start = ((bf16[18,64,128]{2,0,1:T(8,128)(2,1)}), bf16[18,64,128]{2,0,1:T(8,128)(2,1)S(1)}, u32[]{:S(2)}, u32[]{:S(2)}) async-start(bf16[18,64,128]{2,0,1:T(8,128)(2,1)} %copy.12), calls=%async_computation | async-start | bytes 786432 | tf_op jit(solution)/shard_map/all_to_all | solution.py:62
  51.8 74.7 %all-gather.3.cloned.1.call-start = ((), (), s32[]{:S(2)}) async-start(), calls=%async_computation.3 | async-start | bytes 1474560 | tf_op jit(solution)/shard_map/all_gather | solution.py:100
  75.8 13.2 %copy-start.13 = (s32[64,64]{1,0:T(8,128)S(1)}, s32[64,64]{1,0:T(8,128)}, u32[]{:S(2)}) copy-start(s32[64,64]{1,0:T(8,128)} %param.9) | copy-start | bytes 49156
  89.0 19.0 %copy-start.15 = (s32[1,64]{1,0:T(1,128)S(1)}, s32[1,64]{1,0:T(1,128)}, u32[]{:S(2)}) copy-start(s32[1,64]{1,0:T(1,128)} %param.11) | copy-start | bytes 772
  89.0 19.0 %copy-start.16 = (s32[1,64]{1,0:T(1,128)S(1)}, s32[1,64]{1,0:T(1,128)}, u32[]{:S(2)}) copy-start(s32[1,64]{1,0:T(1,128)} %param.10) | copy-start | bytes 772
  97.6 22.9 %all-to-all-start.1 = ((bf16[64,2,1152]{2,1,0:T(2,128)(2,1)}), bf16[64,2,1152]{2,1,0:T(2,128)(2,1)S(1)}, u32[]{:S(2)}, u32[]{:S(2)}) async-start(bf16[64,2,1152]{2,1,0:T(2,128)(2,1)} %copy.14), calls=%async_computation.1 | async-start | bytes 589824 | tf_op jit(solution)/shard_map/all_to_all | solution.py:84
  121.5 184.4 %all-to-all-start.2 = ((bf16[4,1,128,64]{2,3,1,0:T(8,128)(2,1)}), bf16[4,1,128,64]{2,3,1,0:T(8,128)(2,1)S(1)}, u32[]{:S(2)}, u32[]{:S(2)}) async-start(bf16[4,1,128,64]{2,3,1,0:T(8,128)(2,1)} %stack.3228), calls=%async_computation.2 | async-start | bytes 131072 | tf_op jit(solution)/shard_map/all_to_all | solution.py:104
  132.3 3.1 copy-start.12
  135.3 3.1 copy-start.10
  138.4 3.1 copy-start.8
  141.5 3.5 copy-start.6
  145.0 4.9 %copy-start.4 = (bf16[128,128,128]{2,0,1:T(8,128)(2,1)}, bf16[128,128,128]{2,0,1:T(8,128)(2,1)S(1)}, u32[]{:S(2)}) copy-start(bf16[128,128,128]{2,0,1:T(8,128)(2,1)S(1)} %constant_dynamic-update-slice_fusion.384) | copy-start | bytes 12582916
  148.1 81.2 %copy-start.2 = (bf16[128,128,128]{2,0,1:T(8,128)(2,1)}, bf16[128,128,128]{2,0,1:T(8,128)(2,1)S(1)}, u32[]{:S(2)}) copy-start(bf16[128,128,128]{2,0,1:T(8,128)(2,1)S(1)} %constant_dynamic-update-slice_fusion.256) | copy-start | bytes 12582916
  305.9 5.0 %copy-start.11 = (bf16[128,128,128]{2,0,1:T(8,128)(2,1)S(1)}, bf16[128,128,128]{2,0,1:T(8,128)(2,1)}, u32[]{:S(2)}) copy-start(bf16[128,128,128]{2,0,1:T(8,128)(2,1)} %copy-done.10) | copy-start | bytes 12582916
  310.9 3.5 copy-start.9
  314.4 3.5 copy-start.7
  318.0 3.5 copy-start.5
  321.5 3.5 copy-start.3
  337.6 16.4 %copy-start.1 = (bf16[64]{0:T(256)(128)(2,1)S(1)}, bf16[64]{0:T(256)(128)(2,1)}, u32[]{:S(2)}) copy-start(bf16[64]{0:T(256)(128)(2,1)} %param.7) | copy-start | bytes 388
Sparse Core Ops, SparseCore 0:
  92.6 27.0 all-gather.2
